TPU v7x, 256 devices: a whole 4x4x8 slice. The times are simulated.
256 devices in a mesh: group: 16 (over x_lo, z), shard: 16 (over x_hi, y, core).
Axes of the slice: x: 4 (x_hi: 2, x_lo: 2; x = x_hi * 2 + x_lo), y: 4, z: 8, core: 2. Of those that a mesh axis runs over, the one named last changes fastest.
Arguments:
- queries: bfloat16 [2, 3, 32768, 512], P(None, None, ('group', 'shard')), may hold values from -6 to 6
- key_tokens: bfloat16 [2, 3, 32768, 512], P(None, None, ('group', 'shard')), may hold values from -24 to 24
- value_tokens: bfloat16 [2, 3, 32768, 512], P(None, None, ('group', 'shard')), may hold values from -24 to 24
- token_rate: float32 [2, 3, 32768], P(None, None, ('group', 'shard')), may hold values from 0.1 to 1
- state_in: float32 [16, 3, 512, 3, 512], P('group', None, 'shard'), may hold values from -0.25 to 0.25
- init_state: float32 [3, 512, 3, 512], P(None, 'shard'), may hold values from -0.25 to 0.25
- norm_gain: float32 [3, 512], replicated, may hold values from 0.25 to 2.5
Outputs:
- head_output: bfloat16 [2, 3, 32768, 512], P(None, None, ('group', 'shard'))
- state_out: float32 [16, 3, 512, 3, 512], P('group', None, 'shard')
All inputs are finite; a program needn't handle non-finite values.
Results may differ from a plain program's by a relative error of at most 0.011.
Values may be sent and summed in bfloat16 or wider, within the bound.
A program may use at most 128 MiB of HBM per device.

v0:
```python
import jax
import jax.numpy as jnp
from jax import lax
from jax.sharding import PartitionSpec as P

epsilon = 1e-06


def shifted(value, axis, steps):
    count = lax.axis_size(axis)
    leading, last = (max(0, -steps), min(count, count - steps))
    return lax.ppermute(value, axis, [(source, source + steps) for source in range(leading, last)])


def forward(rows, packed):
    pre_gate = jnp.dot(rows, packed[:, 0], preferred_element_type=jnp.float32)
    pre_up = jnp.dot(rows, packed[:, 1], preferred_element_type=jnp.float32)
    sigmoid_gate = jax.nn.sigmoid(pre_gate)
    hidden = (pre_gate * sigmoid_gate * pre_up).astype(jnp.bfloat16)
    produced = lax.dot_general(
        hidden, packed[:, 2], (((1,), (1,)), ((), ())), preferred_element_type=jnp.float32
    )
    return (pre_gate, pre_up, sigmoid_gate, hidden, produced)


def on_device(queries, key_tokens, value_tokens, token_rate, state_in, init_state, norm_gain):
    head_count = queries.shape[1]
    token_rows = queries.shape[2]
    span = token_rows * lax.axis_size("shard")

    def head_pass(slot_index, head_index, packed, shard_weights):
        query_rows = queries[slot_index, head_index]
        key_rows = key_tokens[slot_index, head_index]
        value_rows = value_tokens[slot_index, head_index]
        rate_row = token_rate[slot_index, head_index]
        applied = forward(query_rows, packed)[4]
        normed = (
            applied
            * lax.rsqrt(jnp.mean(applied * applied, axis=-1, keepdims=True) + epsilon)
            * norm_gain[head_index]
        )
        pre_gate, pre_up, sigmoid_gate, hidden, guess = forward(key_rows, packed)
        error = (rate_row[:, None] * (guess - value_rows.astype(jnp.float32))).astype(jnp.bfloat16)
        back_hidden = jnp.dot(error, packed[:, 2], preferred_element_type=jnp.float32)
        grad_gate = (
            back_hidden * pre_up * sigmoid_gate * (1.0 + pre_gate * (1.0 - sigmoid_gate))
        ).astype(jnp.bfloat16)
        grad_up = (back_hidden * pre_gate * sigmoid_gate).astype(jnp.bfloat16)
        contract = (((0,), (0,)), ((), ()))
        gate_part = lax.dot_general(
            key_rows, grad_gate, contract, preferred_element_type=jnp.float32
        )
        up_part = lax.dot_general(key_rows, grad_up, contract, preferred_element_type=jnp.float32)
        down_part = lax.dot_general(error, hidden, contract, preferred_element_type=jnp.float32)
        summed = lax.psum_scatter(
            jnp.stack([gate_part, up_part, down_part], axis=1),
            "shard",
            scatter_dimension=0,
            tiled=True,
        )
        updated = shard_weights - summed / float(span)
        return (normed.astype(jnp.bfloat16), updated)

    def slot_pass(slot_index, shards):
        outputs = []
        updates = []
        arrivals = []
        for head_index in range(head_count):
            packed = lax.all_gather(
                shards[head_index].astype(jnp.bfloat16), "shard", axis=0, tiled=True
            )
            normed, updated = head_pass(slot_index, head_index, packed, shards[head_index])
            outputs.append(normed)
            updates.append(updated)
        return (outputs, updates, arrivals)

    first_outputs, middle, arrivals = slot_pass(0, state_in[0])
    arrived = shifted(jnp.stack(middle, axis=0).astype(jnp.bfloat16), "group", 1).astype(
        jnp.float32
    )
    arrived = jnp.where(lax.axis_index("group") == 0, init_state, arrived)
    second_outputs, final, unused = slot_pass(1, arrived)
    head_output = jnp.stack(
        [jnp.stack(first_outputs, axis=0), jnp.stack(second_outputs, axis=0)], axis=0
    )
    state_out = jnp.stack(final, axis=0)[None]
    return (head_output, state_out)


def solution(mesh):
    in_specs = (
        P(None, None, ("group", "shard"), None),
        P(None, None, ("group", "shard"), None),
        P(None, None, ("group", "shard"), None),
        P(None, None, ("group", "shard")),
        P("group", None, "shard", None, None),
        P(None, "shard", None, None),
        P(),
    )
    out_specs = (P(None, None, ("group", "shard"), None), P("group", None, "shard", None, None))
    return jax.shard_map(
        on_device, mesh=mesh, in_specs=in_specs, out_specs=out_specs, check_vma=False
    )
```

profile of v0, /device:TPU:10, one launch (start us, length us, event | category | flops | bytes accessed | tf_op | source)
XLA Modules:
  0.0 750.2 jit_solution(18101220173649434521)
XLA Ops:
  7.2 1.9 bitcast_convert_fusion.2
  11.4 52.1 %all-gather.9.cloned.1.call-done = bf16[512,3,512]{2,0,1:T(8,128)(2,1)} async-done(((bf16[32,3,512]{2,0,1:T(8,128)(2,1)}), bf16[512,3,512]{2,0,1:T(8,128)(2,1)}) %all-gather.9.cloned.1.call-update) | async-done | bytes 1572880 | tf_op jit(solution)/shard_map/all_gather | solution.py:69
  63.5 1.4 fusion.30
  68.8 48.0 %all-gather.11.cloned.1.call-done = bf16[512,3,512]{2,0,1:T(8,128)(2,1)} async-done(((bf16[32,3,512]{2,0,1:T(8,128)(2,1)}), bf16[512,3,512]{2,0,1:T(8,128)(2,1)}) %all-gather.11.cloned.1.call-update) | async-done | bytes 1572880 | tf_op jit(solution)/shard_map/all_gather | solution.py:69
  116.8 1.4 fusion.33
  127.8 42.3 %all-gather.7.cloned.1.call-done = bf16[512,3,512]{2,0,1:T(8,128)(2,1)} async-done(((bf16[32,3,512]{2,0,1:T(8,128)(2,1)}), bf16[512,3,512]{2,0,1:T(8,128)(2,1)}) %all-gather.7.cloned.1.call-update) | async-done | bytes 1572880 | tf_op jit(solution)/shard_map/all_gather | solution.py:69
  170.1 1.4 fusion.27
  175.6 3.5 copy.30
  179.2 2.2 pad_maximum_fusion.2
  181.3 3.6 copy.36
  184.9 2.2 pad_maximum_fusion.1
  187.1 3.6 copy.33
  192.5 174.8 %all-reduce.13.cloned.1.call-done = (f32[512,3,512]{2,1,0:T(4,128)}, f32[512,3,512]{2,1,0:T(4,128)}, f32[512,3,512]{2,1,0:T(4,128)}) async-done(((f32[512,3,512]{2,1,0:T(4,128)}, f32[512,3,512]{2,1,0:T(4,128)}, f32[512,3,512]{2,1,0:T(4,128)}), (f32[512,3,512]{2,1,0:T(4,128)}, f32[512,3,512]{2,1,0:T(4,128)}, f32[512,3,512]{2,1,0:T(4,128)})) %all-reduce.13.cloned.1.call-update) | async-done | bytes 9437200
  369.8 3.6 collective-permute-start
  373.4 7.3 collective-permute-done
  384.0 52.0 %all-gather.15.cloned.1.call-done = bf16[512,3,512]{2,0,1:T(8,128)(2,1)} async-done(((bf16[32,3,512]{2,0,1:T(8,128)(2,1)}), bf16[512,3,512]{2,0,1:T(8,128)(2,1)}) %all-gather.15.cloned.1.call-update) | async-done | bytes 1572880 | tf_op jit(solution)/shard_map/all_gather | solution.py:69
  436.0 1.4 convolution_bitcast_fusion.21
  441.2 47.4 %all-gather.17.cloned.1.call-done = bf16[512,3,512]{2,0,1:T(8,128)(2,1)} async-done(((bf16[32,3,512]{2,0,1:T(8,128)(2,1)}), bf16[512,3,512]{2,0,1:T(8,128)(2,1)}) %all-gather.17.cloned.1.call-update) | async-done | bytes 1572880 | tf_op jit(solution)/shard_map/all_gather | solution.py:69
  499.6 42.3 %all-gather.13.cloned.1.call-done = bf16[512,3,512]{2,0,1:T(8,128)(2,1)} async-done(((bf16[32,3,512]{2,0,1:T(8,128)(2,1)}), bf16[512,3,512]{2,0,1:T(8,128)(2,1)}) %all-gather.13.cloned.1.call-update) | async-done | bytes 1572880 | tf_op jit(solution)/shard_map/all_gather | solution.py:69
  541.9 1.4 convolution_bitcast_fusion.23
  547.4 3.5 copy.44
  550.9 2.2 pad_maximum_fusion.5
  553.1 3.6 copy.54
  556.7 2.2 pad_maximum_fusion.4
  558.8 3.6 copy.49
  565.0 2.2 multiply_reduce_fusion.4
  568.3 2.2 multiply_reduce_fusion.3
  571.6 2.2 multiply_reduce_fusion.5
  575.0 2.2 multiply_reduce_fusion.1
  578.4 2.2 multiply_reduce_fusion
  581.8 1.5 multiply_reduce_fusion.2
  584.8 154.5 %all-reduce.11.cloned.1.call-done = (f32[512,3,512]{2,1,0:T(4,128)}, f32[512,3,512]{2,1,0:T(4,128)}, f32[512,3,512]{2,1,0:T(4,128)}) async-done(((f32[512,3,512]{2,1,0:T(4,128)}, f32[512,3,512]{2,1,0:T(4,128)}, f32[512,3,512]{2,1,0:T(4,128)}), (f32[512,3,512]{2,1,0:T(4,128)}, f32[512,3,512]{2,1,0:T(4,128)}, f32[512,3,512]{2,1,0:T(4,128)})) %all-reduce.11.cloned.1.call-update) | async-done | bytes 9437200
  (137 shorter events, 59.4 us)
Async XLA Ops:
  7.2 57.8 %copy-start = (bf16[2,3,128,512]{3,2,1,0:T(8,128)(2,1)S(1)}, bf16[2,3,128,512]{3,2,1,0:T(8,128)(2,1)}, u32[]{:S(2)}) copy-start(bf16[2,3,128,512]{3,2,1,0:T(8,128)(2,1)} %param.8) | copy-start | bytes 2359300
  7.2 56.3 %all-gather.9.cloned.1.call-start = ((), (), s32[]{:S(2)}) async-start(), calls=%async_computation.1 | async-start | bytes 1671168 | tf_op jit(solution)/shard_map/all_gather | solution.py:69
  9.1 107.7 %all-gather.11.cloned.1.call-start = ((), (), s32[]{:S(2)}) async-start(), calls=%async_computation.2 | async-start | bytes 1671168 | tf_op jit(solution)/shard_map/all_gather | solution.py:69
  9.9 160.2 %all-gather.7.cloned.1.call-start = ((), (), s32[]{:S(2)}) async-start(), calls=%async_computation | async-start | bytes 1671168 | tf_op jit(solution)/shard_map/all_gather | solution.py:69
  10.6 356.7 %all-reduce.13.cloned.1.call-start = ((), (), s32[]{:S(2)}) async-start(), calls=%async_computation.7 | async-start | bytes 25165824
  63.5 2.7 copy-start.4
  116.8 2.7 copy-start.6
  170.1 2.7 copy-start.8
  190.6 178.8 %copy-start.16 = (f32[1,3,32,3,512]{4,2,3,1,0:T(8,128)S(1)}, f32[1,3,32,3,512]{4,2,3,1,0:T(8,128)}, u32[]{:S(2)}) copy-start(f32[1,3,32,3,512]{4,2,3,1,0:T(8,128)} %param.11) | copy-start | bytes 1769476
  190.7 245.4 %all-gather.15.cloned.1.call-start = ((), (), s32[]{:S(2)}) async-start(), calls=%async_computation.4 | async-start | bytes 1671168 | tf_op jit(solution)/shard_map/all_gather | solution.py:69
  368.3 12.5 %copy-start.17 = (f32[3,32,3,512]{3,1,2,0:T(8,128)S(1)}, f32[3,32,3,512]{3,1,2,0:T(8,128)}, u32[]{:S(2)}) copy-start(f32[3,32,3,512]{3,1,2,0:T(8,128)} %param.12) | copy-start | bytes 1769476
  369.8 66.3 %copy-start.1 = (bf16[2,3,128,512]{3,2,1,0:T(8,128)(2,1)S(1)}, bf16[2,3,128,512]{3,2,1,0:T(8,128)(2,1)}, u32[]{:S(2)}) copy-start(bf16[2,3,128,512]{3,2,1,0:T(8,128)(2,1)} %param.8) | copy-start | bytes 2359300
  369.8 10.9 %collective-permute-start = (bf16[3,32,3,512]{3,1,2,0:T(8,128)(2,1)S(1)}, bf16[3,32,3,512]{3,1,2,0:T(8,128)(2,1)S(1)}, u32[]{:S(2)}, u32[]{:S(2)}) collective-permute-start(bf16[3,32,3,512]{3,1,2,0:T(8,128)(2,1)S(1)} %pad_maximum_fusion.7), channel_id=1, source_target_pairs={{0,16},{16,32},{32,48},{48,64},{64,80},{80,96},{96,112},{112,128},... | collective-permute-start | bytes 884744 | tf_op jit(solution)/shard_map/ppermute | solution.py:12
  380.9 0.8 copy-start.2
  382.4 106.2 %all-gather.17.cloned.1.call-start = ((), (), s32[]{:S(2)}) async-start(), calls=%async_computation.5 | async-start | bytes 1671168 | tf_op jit(solution)/shard_map/all_gather | solution.py:69
  383.0 158.9 %all-gather.13.cloned.1.call-start = ((), (), s32[]{:S(2)}) async-start(), calls=%async_computation.3 | async-start | bytes 1671168 | tf_op jit(solution)/shard_map/all_gather | solution.py:69
  383.8 355.5 %all-reduce.11.cloned.1.call-start = ((), (), s32[]{:S(2)}) async-start(), calls=%async_computation.6 | async-start | bytes 25165824
  436.0 2.7 copy-start.10
  488.6 2.7 copy-start.12
  541.9 2.7 copy-start.14
  562.4 1.4 copy-start.5
  565.0 2.2 copy-start.7
  568.3 2.2 copy-start.9
  571.6 2.2 copy-start.11
  575.0 2.2 copy-start.13
  578.4 2.2 copy-start.15
  581.7 1.6 copy-start.20
  581.7 1.6 copy-start.22
  581.7 1.7 copy-start.19
  581.8 1.7 copy-start.21
  581.8 1.8 copy-start.18
  583.8 158.5 %copy-start.3 = (f32[3,32,3,512]{3,1,2,0:T(8,128)S(1)}, f32[3,32,3,512]{3,1,2,0:T(8,128)}, u32[]{:S(2)}) copy-start(f32[3,32,3,512]{3,1,2,0:T(8,128)} %copy-done.2) | copy-start | bytes 1769476
  (2 other events, 1.4 us)
Sparse Core Ops, SparseCore 0:
  10.8 52.6 all-gather.8
  66.9 49.8 all-gather.10
  120.2 49.8 all-gather.6
  190.8 176.4 all-reduce.12
  382.6 53.4 all-gather.14
  438.7 49.8 all-gather.16
  492.0 49.8 all-gather.12
  562.5 176.6 all-reduce.10
where the time goes:
time: 757 us; the launch traced here: 750 us
  waiting for transfers between devices  623 us (82%)
  matrix products  62 us (8%)
  local copies, waits for them, and re-layouts  33.3 us (4%)
  between operations  15.4 us (2%)
  other arithmetic  12.2 us (2%)
    unnamed x10, waiting for transfers between devices  332 us
    all_gather x6, waiting for transfers between devices, slot_pass(): lax.all_gather(shards[head_index].astype(jnp.bfloat16), 'shard', axis=0,...  284 us
    another operation x6, local copies, waits for them, and re-layouts, head_pass(): jnp.stack([gate_part, up_part, down_part], axis=1)  21.3 us
    dot_general x12, matrix products, forward(): lax.dot_general(hidden, packed[:, 2], (((1,), (1,)), ((), ())), preferred...  19.7 us
    dot_general x12, matrix products, forward(): pre_gate = jnp.dot(rows, packed[:, 0], preferred_element_type=jnp.float32)  15.2 us
  transfers between devices with their start and end apart: 9, of which 9 were waited for; matrix products, arithmetic and copies ran while one was open for 7% of the time, Pallas kernels for 0%

commit v1 on v0

v1 whole, which is shorter than its diff:
```python
import functools

import jax
import jax.numpy as jnp
from jax import lax
from jax.experimental import pallas as pl
from jax.experimental.pallas import tpu as pltpu
from jax.sharding import PartitionSpec as P

MESH = pl.DeviceIdType.MESH
epsilon = 1e-06
f32, bf16 = jnp.float32, jnp.bfloat16

GAP = 5
LAG = {
    "issue": -1, "own": 1, "pair": 0, "across": 1, "gathered": 2, "compute": 2,
    "chip": 3, "ring1": 4, "ring2": 4, "update": 6,
}
ORDER = ("ring1", "update", "issue", "gathered", "own", "across", "pair", "chip", "compute", "ring2")
COPIES = 27


def kernel(
    heads, groups,
    q_hbm, k_hbm, v_hbm, rate_hbm, state_hbm, init_hbm, gain_ref,
    out_ref, state_out_ref,
    q, k, v, rate, init, cur, w, grad, acc, fin, last, moved, land_c, land_y, land_x, land_s,
    in_sem, send_sem, recv_sem,
):
    g = lax.axis_index("group")
    me = lax.axis_index("shard")
    x, y, c = me // 8, (me // 2) % 4, me % 2
    xo, co = 1 - x, 1 - c
    yp, ym, yo = (y + 1) % 4, (y + 3) % 4, (y + 2) % 4
    up, down = (g, x * 8 + yp * 2 + c), (g, x * 8 + ym * 2 + c)
    pair, sib = (g, xo * 8 + y * 2 + c), (g, x * 8 + y * 2 + co)
    ahead, behind = ((g + 1) % groups, me), ((g + groups - 1) % groups, me)
    jobs = 2 * heads
    rows = w.shape[5]
    half = rows // 2
    A, B, ALL = pl.ds(0, half), pl.ds(half, half), pl.ds(0, rows)

    def W(j, px, py, pc, part=ALL):
        return w.at[j, :, px, py, pc, part, :]

    def C(j, py, part=ALL):
        return acc.at[j, :, :, py, part, :]

    def table(n, j):
        if n < 16:
            sent = {
                0: (W(j, x, y, c), up, W(j, x, ym, c)),
                1: (W(j, x, y, c), down, W(j, x, yp, c)),
                2: (W(j, x, y, c), pair, W(j, xo, y, c)),
                3: (W(j, x, y, c), sib, W(j, x, y, co)),
                4: (W(j, xo, y, c), up, W(j, xo, ym, c)),
                5: (W(j, xo, y, c), down, W(j, xo, yp, c)),
                6: (W(j, xo, y, c), sib, W(j, xo, y, co)),
                7: (W(j, x, ym, c, A), up, W(j, x, yo, c, A)),
                8: (W(j, x, yp, c, B), down, W(j, x, yo, c, B)),
                9: (W(j, x, ym, c), sib, W(j, x, ym, co)),
                10: (W(j, x, yp, c), sib, W(j, x, yp, co)),
                11: (W(j, xo, ym, c, A), up, W(j, xo, yo, c, A)),
                12: (W(j, xo, yp, c, B), down, W(j, xo, yo, c, B)),
                13: (W(j, xo, ym, c), sib, W(j, xo, ym, co)),
                14: (W(j, xo, yp, c), sib, W(j, xo, yp, co)),
                15: (w.at[j, :, :, yo, c], sib, w.at[j, :, :, yo, co]),
            }[n]
            return sent[0], sent[0], sent[1], sent[2]
        if n < 19:
            m = n - 16
            return grad.at[j, m, :, :, co], land_c.at[j, m], sib, land_c.at[j, m]
        if n < 25:
            src, to = {
                19: (C(j, yo, A), up), 20: (C(j, yo, B), down),
                21: (C(j, yp, B), up), 22: (C(j, ym, A), down),
                23: (C(j, yp, A), up), 24: (C(j, ym, B), down),
            }[n]
            return src, land_y.at[j, n - 19], to, land_y.at[j, n - 19]
        if n == 25:
            return last.at[j], land_x.at[j], pair, land_x.at[j]
        return moved.at[j], land_s.at[j], ahead, land_s.at[j]

    def copy(n, j):
        src, dst, to, here = table(n, j)
        return pltpu.make_async_remote_copy(
            src_ref=src, dst_ref=dst, send_sem=send_sem.at[j, n], recv_sem=recv_sem.at[j, n],
            device_id=to, device_id_type=MESH,
        )

    def send(j, *which):
        for n in which:
            copy(n, j).start()

    def arrived(j, *which):
        for n in which:
            src, dst, to, here = table(n, j)
            pltpu.make_async_remote_copy(
                src_ref=here, dst_ref=here, send_sem=send_sem.at[j, n], recv_sem=recv_sem.at[j, n],
                device_id=to, device_id_type=MESH,
            ).wait_recv()

    def issue(j):
        arrived(j - heads, 26)
        start = jnp.where(g == 0, init[j - heads], land_s[j - heads].astype(f32))
        cur[j] = start
        w[j, :, x, y, c] = start.astype(bf16)
        send(j, 0, 1, 2, 3)

    def own(j):
        arrived(j, 0, 1)
        send(j, 7, 8, 9, 10)

    def from_pair(j):
        arrived(j, 2)
        send(j, 4, 5, 6)

    def across(j):
        arrived(j, 4, 5)
        send(j, 11, 12, 13, 14)

    def gathered(j):
        arrived(j, 7, 8, 11, 12)
        send(j, 15)

    def compute(j):
        arrived(j, 3, 6, 9, 10, 13, 14, 15)
        tokens, depth = q.shape[1], q.shape[2]

        def weight(m):
            return w[j, m].reshape(depth, w.shape[6])

        both = jnp.concatenate([q[j], k[j]], axis=0)
        gate = jnp.dot(both, weight(0), preferred_element_type=f32)
        value = jnp.dot(both, weight(1), preferred_element_type=f32)
        sig = jax.nn.sigmoid(gate)
        hidden = (gate * sig * value).astype(bf16)
        made = lax.dot_general(hidden, weight(2), (((1,), (1,)), ((), ())), preferred_element_type=f32)
        applied, guess = made[:tokens], made[tokens:]
        scale = jnp.broadcast_to(rate[j], (depth, tokens)).T
        error = (scale * (guess - v[j].astype(f32))).astype(bf16)
        back = jnp.dot(error, weight(2), preferred_element_type=f32)
        pg, pu, ps = gate[tokens:], value[tokens:], sig[tokens:]
        d_gate = (back * pu * ps * (1.0 + pg * (1.0 - ps))).astype(bf16)
        d_up = (back * pg * ps).astype(bf16)
        key_t, err_t = k[j].T, error.T
        for m, (left, right) in enumerate(((key_t, d_gate), (key_t, d_up), (err_t, hidden[tokens:]))):
            part = jnp.dot(left, right, preferred_element_type=f32)
            grad[j, m] = part.astype(bf16).reshape(grad.shape[2:])
            send(j, 16 + m)
        mean = jnp.mean(applied * applied, axis=-1, keepdims=True)
        normed = applied * lax.rsqrt(mean + epsilon) * gain_ref[lax.rem(j, heads)]
        out_ref[j] = normed.astype(bf16)

    def chip(j):
        for m in range(3):
            arrived(j, 16 + m)
            acc[j, m] = (grad[j, m, :, :, c].astype(f32) + land_c[j, m].astype(f32)).astype(bf16)
        send(j, 19, 20, 21, 22)

    def ring1(j):
        arrived(j, 19)
        acc[j, :, :, yp, A] = (acc[j, :, :, yp, A].astype(f32) + land_y[j, 0].astype(f32)).astype(bf16)
        send(j, 23)
        arrived(j, 20)
        acc[j, :, :, ym, B] = (acc[j, :, :, ym, B].astype(f32) + land_y[j, 1].astype(f32)).astype(bf16)
        send(j, 24)

    def ring2(j):
        arrived(j, 21, 22, 23, 24)

        def total(px):
            first = acc[j, :, px, y, A].astype(f32) + land_y[j, 3, :, px].astype(f32) + land_y[j, 4, :, px].astype(f32)
            second = acc[j, :, px, y, B].astype(f32) + land_y[j, 2, :, px].astype(f32) + land_y[j, 5, :, px].astype(f32)
            return jnp.concatenate([first, second], axis=1)

        last[j] = total(xo).astype(bf16)
        send(j, 25)
        fin[j] = total(x)

    def update(j):
        arrived(j, 25)
        new = cur[j] - (fin[j] + land_x[j].astype(f32)) * (1.0 / float(q.shape[1] * 16))

        @pl.when(j < heads)
        def _():
            moved[j] = new.astype(bf16)
            send(j, 26)

        @pl.when(j >= heads)
        def _():
            state_out_ref[j - heads] = new

    def load(n, src, dst):
        return pltpu.make_async_copy(src, dst, in_sem.at[n])

    loads = [
        load(0, state_hbm, cur.at[pl.ds(0, heads)]), load(1, q_hbm, q), load(2, k_hbm, k), load(3, v_hbm, v),
        load(4, rate_hbm, rate), load(5, init_hbm, init),
    ]
    for one in loads:
        one.start()
    barrier = pltpu.get_barrier_semaphore()
    for other in (up, down, pair, sib, ahead, behind):
        pl.semaphore_signal(barrier, inc=1, device_id=other, device_id_type=MESH)
    loads[0].wait()
    for h in range(heads):
        w[h, :, x, y, c] = cur[h].astype(bf16)
    pl.semaphore_wait(barrier, 6)
    for h in range(heads):
        send(h, 0, 1, 2, 3)
    for one in loads[1:]:
        one.wait()

    stages = {
        "issue": issue, "own": own, "pair": from_pair, "across": across, "gathered": gathered, "compute": compute,
        "chip": chip, "ring1": ring1, "ring2": ring2, "update": update,
    }

    def tick(t, carry):
        for name in ORDER:
            step = t - LAG[name]
            second = step >= heads
            j = jnp.where(second, step - GAP, step)
            good = (step >= 0) & ((step < heads) | ((j >= heads) & (j < jobs)))
            if name == "issue":
                good = good & second

            @pl.when(good)
            def _(name=name, j=j):
                stages[name](j)

        return carry

    lax.fori_loop(0, jobs + GAP + max(LAG.values()), tick, 0)

    def drain(j, carry):
        for n in range(COPIES - 1):
            copy(n, j).wait_send()
        return carry

    lax.fori_loop(0, jobs, drain, 0)
    for h in range(heads):
        copy(26, h).wait_send()


def on_device(queries, key_tokens, value_tokens, token_rate, state_in, init_state, norm_gain):
    slots, heads, tokens, depth = queries.shape
    rows, hidden = init_state.shape[1], init_state.shape[3]
    jobs = slots * heads
    groups = lax.axis_size("group")
    half = rows // 2
    state = jnp.transpose(state_in[0], (0, 2, 1, 3))
    init = jnp.transpose(init_state, (0, 2, 1, 3))
    any_spec, vmem = pl.BlockSpec(memory_space=pl.ANY), pl.BlockSpec(memory_space=pltpu.VMEM)
    V = pltpu.VMEM
    out, new = pl.pallas_call(
        functools.partial(kernel, heads, groups),
        out_shape=(
            jax.ShapeDtypeStruct((jobs, tokens, depth), bf16),
            jax.ShapeDtypeStruct((heads, 3, rows, hidden), f32),
        ),
        in_specs=[any_spec] * 6 + [vmem],
        out_specs=(vmem, vmem),
        scratch_shapes=[
            V((jobs, tokens, depth), bf16), V((jobs, tokens, depth), bf16), V((jobs, tokens, depth), bf16),
            V((jobs, 1, tokens), f32), V((heads, 3, rows, hidden), f32), V((jobs, 3, rows, hidden), f32),
            V((jobs, 3, 2, 4, 2, rows, hidden), bf16), V((jobs, 3, 2, 4, 2, rows, hidden), bf16),
            V((jobs, 3, 2, 4, rows, hidden), bf16), V((jobs, 3, rows, hidden), f32),
            V((jobs, 3, rows, hidden), bf16), V((heads, 3, rows, hidden), bf16),
            V((jobs, 3, 2, 4, rows, hidden), bf16), V((jobs, 6, 3, 2, half, hidden), bf16),
            V((jobs, 3, rows, hidden), bf16), V((heads, 3, rows, hidden), bf16),
            pltpu.SemaphoreType.DMA((6,)), pltpu.SemaphoreType.DMA((jobs, COPIES)),
            pltpu.SemaphoreType.DMA((jobs, COPIES)),
        ],
        compiler_params=pltpu.CompilerParams(
            collective_id=0, has_side_effects=True, vmem_limit_bytes=60 * 1024 * 1024
        ),
    )(
        queries.reshape(jobs, tokens, depth), key_tokens.reshape(jobs, tokens, depth),
        value_tokens.reshape(jobs, tokens, depth), token_rate.reshape(jobs, 1, tokens), state, init,
        norm_gain.reshape(heads, 1, depth),
    )
    return out.reshape(queries.shape), jnp.transpose(new, (0, 2, 1, 3))[None]


def solution(mesh):
    in_specs = (
        P(None, None, ("group", "shard"), None),
        P(None, None, ("group", "shard"), None),
        P(None, None, ("group", "shard"), None),
        P(None, None, ("group", "shard")),
        P("group", None, "shard", None, None),
        P(None, "shard", None, None),
        P(),
    )
    out_specs = (P(None, None, ("group", "shard"), None), P("group", None, "shard", None, None))
    return jax.shard_map(
        on_device, mesh=mesh, in_specs=in_specs, out_specs=out_specs, check_vma=False
    )
```

time: 757 us -> 115 us (0.15)
  waiting for transfers between devices: 623 us -> 0 us
  Pallas kernels: 0 us -> 108 us
  matrix products: 62 us -> 0 us
  local copies, waits for them, and re-layouts: 33.3 us -> 4.84 us
  between operations: 15.4 us -> 0.67 us
  other arithmetic: 12.2 us -> 0 us
    unnamed x10 -> x0, waiting for transfers between devices: 332 us -> none
    all_gather x6 -> x0, waiting for transfers between devices: 284 us -> none  [slot_pass(): lax.all_gather(shards[head_index].astype(jnp.bfloat16), 'shard', axis=0,...]
    pallas_call x0 -> x1, Pallas kernels: none -> 108 us  [on_device(): pl.pallas_call(functools.partial(kernel, heads, groups), out_shape=(jax.S...]
    dot_general x54 -> x0, matrix products: 62 us -> none  [the longest x12 19.7 us: forward(): lax.dot_general(hidden, packed[:, 2], (((1,), (1,)), ((), ())), preferred...]
    another operation x6 -> x0, local copies, waits for them, and re-layouts: 21.3 us -> none  [head_pass(): jnp.stack([gate_part, up_part, down_part], axis=1)]
    another operation x15 -> x0, other arithmetic: 11.2 us -> none  [the longest x6 9.26 us: head_pass(): jnp.stack([gate_part, up_part, down_part], axis=1)]
  transfers between devices with their start and end apart: 9 -> 0, of which waited for: 9 -> 0; matrix products, arithmetic and copies ran while one was open for 7% -> 0% of each run, Pallas kernels for 0% -> 0%
where the time goes in v1:
time: 115 us; the launch traced here: 113 us
  Pallas kernels  108 us (94%)
  local copies, waits for them, and re-layouts  4.84 us (4%)
    pallas_call x1, Pallas kernels, on_device(): pl.pallas_call(functools.partial(kernel, heads, groups), out_shape=(jax.S...  108 us
    unnamed x9, local copies, waits for them, and re-layouts  3.65 us

profile of v1, /device:TPU:10, one launch (start us, length us, event | category | flops | bytes accessed | tf_op | source)
XLA Modules:
  0.0 113.2 jit_solution(8522397790552108495)
XLA Ops:
  0.6 0.0 copy-start.2
  0.6 0.0 copy-start.1
  0.6 0.7 copy-done.2
  1.3 0.6 reshape.28.rate_hbm
  1.9 0.0 copy-done.1
  1.9 0.6 reshape.26.gain_ref
  2.5 107.7 %shard_map.86 = (bf16[6,128,512]{2,1,0:T(8,128)(2,1)}, f32[3,3,32,512]{3,2,1,0:T(8,128)}) custom-call(bf16[6,128,512]{2,1,0:T(8,128)(2,1)} %bitcast.12, bf16[6,128,512]{2,1,0:T(8,128)(2,1)} %bitcast.13, bf16[6,128,512]{2,1,0:T(8,128)(2,1)} %bitcast.14, f32[6,1,128]{2,1,0:T(1,128)} %reshape.28.rate_hbm, f32[3,3,32,512]{3,2,1,0:T(8,128)} %bitcast.16, ...), custom_call_target="tpu_custom_call" | custom-call | tf_op jit(solution)/shard_map/pallas_call | solution.py:257
  110.2 0.0 copy-start
  110.2 2.2 %copy.14 = bf16[2,3,128,512]{3,2,1,0:T(8,128)(2,1)} copy(bf16[2,3,128,512]{3,2,1,0:T(8,128)(2,1)} %bitcast.11) | data formatting | bytes 1572864
  112.3 0.0 copy-done
  112.3 0.8 copy.15
  (1 shorter events, 0.0 us)
Async XLA Ops:
  0.6 0.7 copy-start.2
  0.6 1.3 %copy-start.1 = (f32[3,512]{1,0:T(4,128)S(1)}, f32[3,512]{1,0:T(4,128)}, u32[]{:S(2)}) copy-start(f32[3,512]{1,0:T(4,128)} %param.13) | copy-start | bytes 18436
  110.2 2.2 %copy-start = (f32[3,3,32,512]{3,2,1,0:T(8,128)S(1)}, f32[3,3,32,512]{3,2,1,0:T(8,128)}, u32[]{:S(2)}) copy-start(f32[3,3,32,512]{3,2,1,0:T(8,128)} %get-tuple-element.5) | copy-start | bytes 1769476

commit v2 on v1

v2 whole, which is shorter than its diff:
```python
import functools

import jax
import jax.numpy as jnp
from jax import lax
from jax.experimental import pallas as pl
from jax.experimental.pallas import tpu as pltpu
from jax.sharding import PartitionSpec as P

MESH = pl.DeviceIdType.MESH
epsilon = 1e-06
f32, bf16 = jnp.float32, jnp.bfloat16

SCHEDULE = (
    "issue0", "issue1", "own0", "pair0", "issue2", "own1", "far0", "across0", "pair1", "farpair0", "own2", "far1",
    "compute0", "far2", "pair2", "across1", "farpair1", "chip0", "compute1", "farpair2", "across2", "rfar0",
    "chip1", "compute2", "rcross0", "relay0", "rfar1", "chip2", "update0", "rcross1", "relay1", "rfar2", "issue3",
    "update1", "rcross2", "relay2", "own3", "issue4", "update2", "pair3", "far3", "own4", "issue5", "across3",
    "farpair3", "far4", "pair4", "compute3", "own5", "across4", "farpair4", "pair5", "far5", "compute4", "chip3",
    "across5", "chip4", "farpair5", "compute5", "rcross3", "rfar3", "chip5", "rcross4", "rfar4", "rfar5",
    "rcross5", "relay3", "relay4", "relay5", "update4", "update3", "update5",
)
COPIES = 30


def kernel(
    heads, groups,
    q_hbm, k_hbm, v_hbm, rate_hbm, state_hbm, init_hbm, gain_hbm,
    out_ref, state_out_ref,
    q, k, v, rate, init, gain, cur, w, grad, acc, moved, land_c, land_p, land_x, land_y, land_l, land_s,
    in_sem, send_sem, recv_sem, go_sem,
):
    g = lax.axis_index("group")
    me = lax.axis_index("shard")
    x, y, c = me // 8, (me // 2) % 4, me % 2
    xo, co = 1 - x, 1 - c
    yp, ym, yo = (y + 1) % 4, (y + 3) % 4, (y + 2) % 4
    up, down = (g, x * 8 + yp * 2 + c), (g, x * 8 + ym * 2 + c)
    pair, sib = (g, xo * 8 + y * 2 + c), (g, x * 8 + y * 2 + co)
    ahead, behind = ((g + 1) % groups, me), ((g + groups - 1) % groups, me)
    middle = groups // 2 - 1
    jobs = 2 * heads
    rows = w.shape[5]
    half = rows // 2
    A, B, ALL = pl.ds(0, half), pl.ds(half, half), pl.ds(0, rows)

    def W(j, px, py, pc, part=ALL):
        return w.at[j, :, px, py, pc, part, :]

    def R(j, px, py, part=ALL):
        return acc.at[j, :, px, py, part, :]

    def table(n, j):
        if n < 16:
            sent, to, here = {
                0: (W(j, x, y, c), up, W(j, x, ym, c)),
                1: (W(j, x, y, c), down, W(j, x, yp, c)),
                2: (W(j, x, y, c), pair, W(j, xo, y, c)),
                3: (W(j, x, y, c), sib, W(j, x, y, co)),
                4: (W(j, xo, y, c), up, W(j, xo, ym, c)),
                5: (W(j, xo, y, c), down, W(j, xo, yp, c)),
                6: (W(j, xo, y, c), sib, W(j, xo, y, co)),
                7: (W(j, x, ym, c, A), up, W(j, x, yo, c, A)),
                8: (W(j, x, yp, c, B), down, W(j, x, yo, c, B)),
                9: (W(j, x, ym, c), sib, W(j, x, ym, co)),
                10: (W(j, x, yp, c), sib, W(j, x, yp, co)),
                11: (W(j, x, yo, c), pair, W(j, xo, yo, c)),
                12: (W(j, xo, yo, c), sib, W(j, xo, yo, co)),
                13: (W(j, xo, ym, c), sib, W(j, xo, ym, co)),
                14: (W(j, xo, yp, c), sib, W(j, xo, yp, co)),
                15: (W(j, x, yo, c), sib, W(j, x, yo, co)),
            }[n]
            return sent, sent, to, here
        if n < 19:
            m = n - 16
            return grad.at[j, m, :, :, co], land_c.at[j, m], sib, land_c.at[j, m]
        if n == 19:
            return R(j, xo, yo), land_p.at[j], pair, land_p.at[j]
        if n < 22:
            src, to = ((R(j, xo, yp), up), (R(j, xo, ym), down))[n - 20]
            return src, land_x.at[j, n - 20], to, land_x.at[j, n - 20]
        if n < 28:
            src, to = (
                (R(j, x, yp, B), up), (R(j, x, ym, A), down), (R(j, x, yo, A), up), (R(j, x, yo, B), down),
                (R(j, x, yp, A), up), (R(j, x, ym, B), down),
            )[n - 22]
            return src, land_y.at[j, n - 22], to, land_y.at[j, n - 22]
        if n == 28:
            return R(j, xo, y), land_l.at[j], pair, land_l.at[j]
        return moved.at[j], land_s.at[j], ahead, land_s.at[j]

    def copy(n, j):
        src, dst, to, here = table(n, j)
        return pltpu.make_async_remote_copy(
            src_ref=src, dst_ref=dst, send_sem=send_sem.at[j, n], recv_sem=recv_sem.at[j, n],
            device_id=to, device_id_type=MESH,
        )

    def send(j, *which):
        for n in which:
            copy(n, j).start()

    def arrived(j, *which):
        for n in which:
            src, dst, to, here = table(n, j)
            pltpu.make_async_remote_copy(
                src_ref=here, dst_ref=here, send_sem=send_sem.at[j, n], recv_sem=recv_sem.at[j, n],
                device_id=to, device_id_type=MESH,
            ).wait_recv()

    def issue(j):
        if j >= heads:
            @pl.when(g == 0)
            def _():
                cur[j] = init[j - heads]
                w[j, :, x, y, c] = init[j - heads].astype(bf16)

            @pl.when(g > 0)
            def _():
                arrived(j - heads, 29)
                cur[j] = land_s[j - heads].astype(f32)
                w[j, :, x, y, c] = land_s[j - heads]

        send(j, 0, 1, 2, 3)

    def own(j):
        arrived(j, 0, 1)
        send(j, 7, 8, 9, 10)

    def from_pair(j):
        arrived(j, 2)
        send(j, 4, 5, 6)

    def far(j):
        arrived(j, 7, 8)
        send(j, 11, 15)

    def across(j):
        arrived(j, 4, 5)
        send(j, 13, 14)

    def far_pair(j):
        arrived(j, 11)
        send(j, 12)

    def compute(j):
        arrived(j, 3, 6, 9, 10, 13, 14, 15, 12)
        tokens, depth = q.shape[1], q.shape[2]
        slot, head = divmod(j, heads)

        def weight(m):
            return w[j, m].reshape(depth, w.shape[6])

        both = jnp.concatenate([q[j], k[j]], axis=0)
        gate = jnp.dot(both, weight(0), preferred_element_type=f32)
        value = jnp.dot(both, weight(1), preferred_element_type=f32)
        sig = jax.nn.sigmoid(gate)
        hidden = (gate * sig * value).astype(bf16)
        made = lax.dot_general(hidden, weight(2), (((1,), (1,)), ((), ())), preferred_element_type=f32)
        applied, guess = made[:tokens], made[tokens:]
        scale = jnp.broadcast_to(rate[head, pl.ds(slot, 1)], (depth, tokens)).T
        error = (scale * (guess - v[j].astype(f32))).astype(bf16)
        back = jnp.dot(error, weight(2), preferred_element_type=f32)
        pg, pu, ps = gate[tokens:], value[tokens:], sig[tokens:]
        d_gate = (back * pu * ps * (1.0 + pg * (1.0 - ps))).astype(bf16)
        d_up = (back * pg * ps).astype(bf16)
        key_t, err_t = k[j].T, error.T
        for m, (left, right) in enumerate(((key_t, d_gate), (key_t, d_up), (err_t, hidden[tokens:]))):
            part = jnp.dot(left, right, preferred_element_type=f32)
            grad[j, m] = part.astype(bf16).reshape(grad.shape[2:])
            send(j, 16 + m)
        mean = jnp.mean(applied * applied, axis=-1, keepdims=True)
        normed = applied * lax.rsqrt(mean + epsilon) * gain[pl.ds(head, 1)]
        out_ref[j] = normed.astype(bf16)

    def chip(j):
        for m in range(3):
            arrived(j, 16 + m)
            acc[j, m] = (grad[j, m, :, :, c].astype(f32) + land_c[j, m].astype(f32)).astype(bf16)
        send(j, 20, 21, 19, 22, 23)

    def r_far(j):
        arrived(j, 19)
        acc[j, :, x, yo] = (acc[j, :, x, yo].astype(f32) + land_p[j].astype(f32)).astype(bf16)
        send(j, 24, 25)

    def r_cross(j):
        arrived(j, 20, 21)
        both = land_x[j, 0].astype(f32) + land_x[j, 1].astype(f32)
        acc[j, :, xo, y] = (acc[j, :, xo, y].astype(f32) + both).astype(bf16)
        send(j, 28)

    def relay(j):
        arrived(j, 24)
        acc[j, :, x, yp, A] = (acc[j, :, x, yp, A].astype(f32) + land_y[j, 2].astype(f32)).astype(bf16)
        send(j, 26)
        arrived(j, 25)
        acc[j, :, x, ym, B] = (acc[j, :, x, ym, B].astype(f32) + land_y[j, 3].astype(f32)).astype(bf16)
        send(j, 27)

    def update(j):
        arrived(j, 22, 23, 26, 27, 28)
        first = land_y[j, 1].astype(f32) + land_y[j, 4].astype(f32)
        second = land_y[j, 0].astype(f32) + land_y[j, 5].astype(f32)
        total = acc[j, :, x, y].astype(f32) + jnp.concatenate([first, second], axis=1) + land_l[j].astype(f32)
        new = cur[j] - total * (1.0 / float(q.shape[1] * 16))

        if j >= heads:
            state_out_ref[j - heads] = new
            return

        @pl.when(g < groups - 1)
        def _():
            moved[j] = new.astype(bf16)
            if j == 0:
                @pl.when(g == middle)
                def _():
                    pl.semaphore_wait(go_sem, 1)
            send(j, 29)

    def load(n, src, dst):
        return pltpu.make_async_copy(src, dst, in_sem.at[n])

    loads = [
        load(0, state_hbm, cur.at[pl.ds(0, heads)]), load(1, q_hbm, q), load(2, k_hbm, k), load(3, v_hbm, v),
        load(4, rate_hbm, rate), load(5, init_hbm, init), load(6, gain_hbm, gain),
    ]
    for one in loads:
        one.start()
    barrier = pltpu.get_barrier_semaphore()

    def hello(other):
        pl.semaphore_signal(barrier, inc=1, device_id=other, device_id_type=MESH)

    for other in (up, down, pair, sib):
        hello(other)

    @pl.when((g > 0) & (g != middle + 1))
    def _():
        hello(behind)

    @pl.when((g == middle) | (g == middle + 1))
    def _():
        hello((groups - 1, me))

    loads[0].wait()
    for h in range(heads):
        w[h, :, x, y, c] = cur[h].astype(bf16)
    near = jnp.where(g == middle, 4, jnp.where(g == groups - 1, 6, 5))
    pl.semaphore_wait(barrier, near)

    @pl.when(g == groups - 1)
    def _():
        pl.semaphore_signal(go_sem, inc=1, device_id=(middle, me), device_id_type=MESH)

    stages = {
        "issue": issue, "own": own, "pair": from_pair, "far": far, "across": across, "farpair": far_pair,
        "compute": compute, "chip": chip, "rfar": r_far, "rcross": r_cross, "relay": relay, "update": update,
    }

    waited = False
    for step in SCHEDULE:
        name, j = step[:-1], int(step[-1])
        if name == "compute" and not waited:
            waited = True
            for one in loads[1:]:
                one.wait()
        stages[name](j)

    def drain(j, carry):
        for n in range(COPIES - 1):
            copy(n, j).wait_send()
        return carry

    lax.fori_loop(0, jobs, drain, 0)

    @pl.when(g < groups - 1)
    def _():
        for h in range(heads):
            copy(COPIES - 1, h).wait_send()


def on_device(queries, key_tokens, value_tokens, token_rate, state_in, init_state, norm_gain):
    slots, heads, tokens, depth = queries.shape
    rows, hidden = init_state.shape[1], init_state.shape[3]
    jobs = slots * heads
    groups = lax.axis_size("group")
    half = rows // 2
    state = jnp.transpose(state_in[0], (0, 2, 1, 3))
    init = jnp.transpose(init_state, (0, 2, 1, 3))
    any_spec, vmem = pl.BlockSpec(memory_space=pl.ANY), pl.BlockSpec(memory_space=pltpu.VMEM)
    V = pltpu.VMEM
    out, new = pl.pallas_call(
        functools.partial(kernel, heads, groups),
        out_shape=(
            pltpu.VMEM((jobs, tokens, depth), bf16),
            pltpu.VMEM((heads, 3, rows, hidden), f32),
        ),
        in_specs=[any_spec] * 7,
        out_specs=(vmem, vmem),
        scratch_shapes=[
            V((jobs, tokens, depth), bf16), V((jobs, tokens, depth), bf16), V((jobs, tokens, depth), bf16),
            V((heads, slots, tokens), f32), V((heads, 3, rows, hidden), f32), V((heads, depth), f32),
            V((jobs, 3, rows, hidden), f32),
            V((jobs, 3, 2, 4, 2, rows, hidden), bf16), V((jobs, 3, 2, 4, 2, rows, hidden), bf16),
            V((jobs, 3, 2, 4, rows, hidden), bf16), V((heads, 3, rows, hidden), bf16),
            V((jobs, 3, 2, 4, rows, hidden), bf16), V((jobs, 3, rows, hidden), bf16),
            V((jobs, 2, 3, rows, hidden), bf16), V((jobs, 6, 3, half, hidden), bf16),
            V((jobs, 3, rows, hidden), bf16), V((heads, 3, rows, hidden), bf16),
            pltpu.SemaphoreType.DMA((7,)), pltpu.SemaphoreType.DMA((jobs, COPIES)),
            pltpu.SemaphoreType.DMA((jobs, COPIES)), pltpu.SemaphoreType.REGULAR,
        ],
        compiler_params=pltpu.CompilerParams(
            collective_id=0, has_side_effects=True, vmem_limit_bytes=60 * 1024 * 1024
        ),
    )(
        queries.reshape(jobs, tokens, depth), key_tokens.reshape(jobs, tokens, depth),
        value_tokens.reshape(jobs, tokens, depth), jnp.transpose(token_rate, (1, 0, 2)), state, init,
        norm_gain,
    )
    return out.reshape(queries.shape), jnp.transpose(new, (0, 2, 1, 3))[None]


def solution(mesh):
    in_specs = (
        P(None, None, ("group", "shard"), None),
        P(None, None, ("group", "shard"), None),
        P(None, None, ("group", "shard"), None),
        P(None, None, ("group", "shard")),
        P("group", None, "shard", None, None),
        P(None, "shard", None, None),
        P(),
    )
    out_specs = (P(None, None, ("group", "shard"), None), P("group", None, "shard", None, None))
    return jax.shard_map(
        on_device, mesh=mesh, in_specs=in_specs, out_specs=out_specs, check_vma=False
    )
```

time: 115 us -> 92.7 us (0.81); the launches traced: 113 us -> 92.7 us
  Pallas kernels: 108 us -> 90.3 us
  local copies, waits for them, and re-layouts: 4.84 us -> 1.7 us
    pallas_call x1, Pallas kernels: 108 us -> 90.3 us  [on_device(): pl.pallas_call(functools.partial(kernel, heads, groups), out_shape=(pltpu...]
    unnamed x9 -> x2, local copies, waits for them, and re-layouts: 3.65 us -> 1.7 us
    reshape x2 -> x0, local copies, waits for them, and re-layouts: 1.19 us -> none  [the longest x1 0.6 us: on_device(): norm_gain.reshape(heads, 1, depth)]
where the time goes in v2:
time: 92.7 us
  Pallas kernels  90.3 us (97%)
  local copies, waits for them, and re-layouts  1.7 us (2%)
    pallas_call x1, Pallas kernels, on_device(): pl.pallas_call(functools.partial(kernel, heads, groups), out_shape=(pltpu...  90.3 us

profile of v2, /device:TPU:10, one launch (start us, length us, event | category | flops | bytes accessed | tf_op | source)
XLA Modules:
  0.0 92.7 jit_solution(12318661374515824145)
XLA Ops:
  0.6 90.3 %shard_map.86 = (bf16[6,128,512]{2,1,0:T(8,128)(2,1)S(1)}, f32[3,3,32,512]{3,2,1,0:T(8,128)S(1)}) custom-call(bf16[6,128,512]{2,1,0:T(8,128)(2,1)} %bitcast.14, bf16[6,128,512]{2,1,0:T(8,128)(2,1)} %bitcast.15, bf16[6,128,512]{2,1,0:T(8,128)(2,1)} %bitcast.16, f32[3,2,128]{2,1,0:T(2,128)} %bitcast.19, f32[3,3,32,512]{3,2,1,0:T(8,128)} %bitcast.17, ...), custom_call_target="tpu_custom_call" | custom-call | tf_op jit(solution)/shard_map/pallas_call | solution.py:293
  91.0 0.9 copy.11
  91.8 0.8 copy.12

commit v3 on v2

v3 whole, which is shorter than its diff:
```python
import functools

import jax
import jax.numpy as jnp
from jax import lax
from jax.experimental import pallas as pl
from jax.experimental.pallas import tpu as pltpu
from jax.sharding import PartitionSpec as P

MESH = pl.DeviceIdType.MESH
epsilon = 1e-06
f32, bf16 = jnp.float32, jnp.bfloat16

(
    U0A, U0B, D0A, D0B, X0A, X0B, S0, F7, F8, S9, S10, BU, BD, U4A, U4B, D5A, D5B, S6, GA, GB, S15, S12, S13, S14,
    C0, C1, C2, H19A, H19B, U20A, U20B, D21A, D21B, PA, PB, U22, D23, U24, D25, X28A, X28B, U26, D27, SHIFT_A,
    SHIFT_B, ISA, ISB, KEYS, QUERIES, CHIP, RFA, RFB, RCA, RCB, RLU, RLD, UPA, UPB, R12, R13, R14
) = range(61)
A, B, AB = range(3)
ALL, GATE, REST = range(3)
UP, DOWN, PAIR, SIB = range(4)
SCHEDULE = (
    2, 26, 0, 32, 20, 1, 18, 31, 25, 19, 44, 8, 50, 14, 80, 30, 49, 73, 43, 92, 86, 98, 7, 42, 68, 74, 13, 110,
    116, 38, 79, 62, 48, 104, 122, 97, 24, 37, 109, 103, 96, 56, 115, 134, 67, 91, 36, 121, 140, 66, 85, 128, 84,
    72, 78, 61, 102, 55, 108, 12, 284, 127, 90, 114, 133, 6, 139, 290, 296, 170, 218, 176, 164, 283, 182, 138, 120,
    188, 132, 54, 60, 206, 126, 194, 200, 212, 308, 230, 295, 169, 217, 175, 193, 163, 205, 302, 224, 282, 181,
    211, 320, 242, 332, 254, 314, 236, 307, 229, 187, 326, 248, 294, 162, 199, 186, 301, 223, 174, 168, 192, 319,
    344, 266, 204, 241, 180, 338, 260, 331, 253, 300, 222, 198, 289, 325, 313, 247, 235, 210, 306, 312, 228, 216,
    234, 318, 343, 265, 324, 246, 281, 35, 240, 23, 337, 259, 275, 5, 330, 252, 29, 17, 11, 336, 258, 53, 89, 77,
    47, 71, 101, 342, 264, 280, 34, 22, 83, 274, 28, 41, 16, 4, 95, 119, 10, 113, 273, 40, 3, 52, 59, 65, 137, 27,
    125, 107, 46, 88, 64, 279, 21, 70, 76, 143, 100, 33, 118, 45, 131, 82, 94, 58, 112, 9, 51, 15, 75, 106, 39,
    287, 111, 124, 99, 105, 142, 69, 136, 81, 130, 87, 117, 93, 123, 299, 57, 185, 167, 197, 63, 215, 286, 191,
    203, 293, 135, 173, 129, 141, 323, 179, 245, 305, 227, 221, 298, 190, 166, 285, 178, 220, 202, 209, 311, 184,
    172, 317, 214, 233, 329, 196, 297, 171, 183, 189, 177, 251, 195, 316, 165, 288, 207, 304, 310, 232, 335, 291,
    226, 322, 201, 208, 239, 309, 231, 257, 219, 315, 244, 303, 225, 321, 238, 292, 243, 213, 237, 328, 334, 250,
    256, 333, 255, 327, 249, 341, 340, 347, 346, 345, 339,
)
GATHER = {
    U0A: (0, 0, A, ALL, UP, ()), U0B: (0, 0, B, ALL, UP, ()),
    D0A: (0, 0, A, ALL, DOWN, ()), D0B: (0, 0, B, ALL, DOWN, ()),
    X0A: (0, 0, A, ALL, PAIR, ()), X0B: (0, 0, B, ALL, PAIR, ()),
    S0: (0, 0, AB, ALL, SIB, ()),
    F7: (0, 3, A, ALL, UP, (U0A,)), F8: (0, 1, B, ALL, DOWN, (D0B,)),
    S9: (0, 3, AB, ALL, SIB, (U0A, U0B)), S10: (0, 1, AB, ALL, SIB, (D0A, D0B)),
    BU: (0, 3, A, GATE, PAIR, (U0A,)), BD: (0, 1, B, GATE, PAIR, (D0B,)),
    U4A: (1, 0, A, REST, UP, (X0A,)), U4B: (1, 0, B, ALL, UP, (X0B,)),
    D5A: (1, 0, A, ALL, DOWN, (X0A,)), D5B: (1, 0, B, REST, DOWN, (X0B,)),
    S6: (1, 0, AB, ALL, SIB, (X0A, X0B)),
    GA: (0, 2, A, ALL, PAIR, (F7,)), GB: (0, 2, B, ALL, PAIR, (F8,)),
    S15: (0, 2, AB, ALL, SIB, (F7, F8)), S12: (1, 2, AB, ALL, SIB, (R12,)),
    S13: (1, 3, AB, ALL, SIB, (R13,)), S14: (1, 1, AB, ALL, SIB, (R14,)),
}
REDUCE = {
    H19A: (1, 2, A, ALL, PAIR), H19B: (1, 2, B, ALL, PAIR),
    U20A: (1, 1, A, REST, UP), U20B: (1, 1, B, ALL, UP),
    D21A: (1, 3, A, ALL, DOWN), D21B: (1, 3, B, REST, DOWN),
    PA: (1, 1, A, GATE, PAIR), PB: (1, 3, B, GATE, PAIR),
    U22: (0, 1, B, ALL, UP), D23: (0, 3, A, ALL, DOWN),
    U24: (0, 2, A, ALL, UP), D25: (0, 2, B, ALL, DOWN),
    X28A: (1, 0, A, ALL, PAIR), X28B: (1, 0, B, ALL, PAIR),
    U26: (0, 1, A, ALL, UP), D27: (0, 3, B, ALL, DOWN),
}
ADD = {
    RFA: (0, 2, A, ((H19A, ALL),)), RFB: (0, 2, B, ((H19B, ALL),)),
    RCA: (1, 0, A, ((D21A, ALL), (U20A, REST))), RCB: (1, 0, B, ((U20B, ALL), (D21B, REST))),
    RLU: (0, 1, A, ((U24, ALL), (PA, GATE))), RLD: (0, 3, B, ((D25, ALL), (PB, GATE))),
}
FINAL = {UPA: (A, (D23, U26, X28A)), UPB: (B, (U22, D27, X28B))}
TERMS = (C0, C1, C2)
SHIFT = (SHIFT_A, SHIFT_B)
WAITS = {
    U0A: (U0A,), U0B: (U0B,), D0A: (D0A,), D0B: (D0B,), X0A: (X0A,), X0B: (X0B,),
    F7: (F7,), F8: (F8,), R12: (GA, GB), R13: (U4A, U4B, BU), R14: (D5A, D5B, BD),
    KEYS: (S0, S9, S10, S6, S15, S12, S13, S14), CHIP: TERMS,
    RFA: (H19A,), RFB: (H19B,), RCA: (D21A, U20A), RCB: (U20B, D21B),
    RLU: (U24, PA), RLD: (D25, PB), UPA: FINAL[UPA][1], UPB: FINAL[UPB][1],
    SHIFT_A: (SHIFT_A,), SHIFT_B: (SHIFT_B,),
}
GROUP = {name: list(WAITS).index(group) for group, names in WAITS.items() for name in names}
SIZE = (3, 1, 2)
PLACE, LANDED = {}, 0
for step in (RFA, RFB, RCA, RCB, RLU, RLD, UPA, UPB):
    for name in WAITS[step]:
        PLACE[name] = (LANDED, SIZE[REDUCE[name][3]])
        LANDED += SIZE[REDUCE[name][3]]
SENT = (
    sum(SIZE[which] * (1, 1, 2)[rows_of] for _, _, rows_of, which, _, _ in GATHER.values())
    + sum(size for _, size in PLACE.values()) + 96
)


def kernel(
    heads, groups,
    q_hbm, k_hbm, v_hbm, rate_hbm, state_hbm, init_hbm, gain_hbm,
    out_ref, state_out_ref,
    q, k, v, rate, init, gain, cur, w, grad, acc, moved, land_c, land,
    in_sem, send_sem, recv_sem, shift_sem, go_sem,
):
    g = lax.axis_index("group")
    me = lax.axis_index("shard")
    x, y, c = me // 8, (me // 2) % 4, me % 2
    xo, co = 1 - x, 1 - c
    yp, ym, yo = (y + 1) % 4, (y + 3) % 4, (y + 2) % 4
    up, down = (g, x * 8 + yp * 2 + c), (g, x * 8 + ym * 2 + c)
    pair, sib = (g, xo * 8 + y * 2 + c), (g, x * 8 + y * 2 + co)
    middle = groups // 2 - 1
    across = xo * 8 + y * 2 + c
    ahead = ((g + 1) % groups, jnp.where(g == middle, across, me))
    behind = ((g + groups - 1) % groups, me)
    jobs = 2 * heads
    rows = w.shape[5]
    half = rows // 2
    part = (pl.ds(0, half), pl.ds(half, half), pl.ds(0, rows))
    mats = (pl.ds(0, 3), pl.ds(0, 1), pl.ds(1, 2))
    column, ring = (x, xo), (y, yp, yo, ym)
    swapped = g == middle + 1
    xs = jnp.where(swapped, xo, x)
    gather_column = ((x, xo),) * heads + ((xs, 1 - xs),) * heads
    to = (up, down, pair, sib)
    origin = ((0, 3), (0, 1), (1, 0), (0, 0))

    def copy(name, j):
        sem = send_sem.at[j]
        if name in GATHER:
            px, py, rows_of, which, way, needs = GATHER[name]
            src = w.at[j, mats[which], gather_column[j][px], ring[py], c, part[rows_of], :]
            dst, target = src, to[way]
        elif name in TERMS:
            m = TERMS.index(name)
            src, dst, target = grad.at[j, m, :, :, co], land_c.at[j, m], sib
        elif name in REDUCE:
            px, py, rows_of, which, way = REDUCE[name]
            src = acc.at[j, mats[which], column[px], ring[py], part[rows_of], :]
            dst, target = land.at[j, pl.ds(*PLACE[name])], to[way]
        else:
            n = SHIFT.index(name)
            src, dst = moved.at[j, :, part[n], :], w.at[j + heads, :, x, y, c, part[n], :]
            target, sem = ahead, shift_sem.at[j, n]
        return pltpu.make_async_remote_copy(
            src_ref=src, dst_ref=dst, send_sem=sem, recv_sem=recv_sem.at[j, GROUP[name]],
            device_id=target, device_id_type=MESH,
        )

    def arrived(j, group):
        names = WAITS[group]
        if group == KEYS:
            place = w.at[j, :, :, :, co]
        elif group == CHIP:
            place = land_c.at[j]
        elif group in SHIFT:
            place = w.at[j + heads, :, xs, y, c, part[SHIFT.index(group)], :]
        elif names[0] in GATHER:
            px, py, rows_of, which, way, needs = GATHER[names[0]]
            px, py = (px + origin[way][0]) % 2, (py + origin[way][1]) % 4
            place = w.at[j, :, gather_column[j][px], ring[py], c, part[rows_of if len(names) == 1 else AB], :]
        else:
            place = land.at[j, pl.ds(PLACE[names[0]][0], sum(PLACE[name][1] for name in names))]
        pltpu.make_async_remote_copy(
            src_ref=place, dst_ref=place, send_sem=send_sem.at[j], recv_sem=recv_sem.at[j, list(WAITS).index(group)],
            device_id=sib, device_id_type=MESH,
        ).wait_recv()

    here = set()

    def need(j, *groups_of):
        for group in groups_of:
            if (group, j) not in here:
                here.add((group, j))
                arrived(j, group)

    def compute(j):
        need(j, KEYS)
        tokens, depth = q.shape[1], q.shape[2]
        slot, head = divmod(j, heads)

        def weight(m):
            return w[j, m].reshape(depth, w.shape[6])

        rows_in = k[j]
        gate = jnp.dot(rows_in, weight(0), preferred_element_type=f32)
        value = jnp.dot(rows_in, weight(1), preferred_element_type=f32)
        sig = jax.nn.sigmoid(gate)
        hidden = (gate * sig * value).astype(bf16)
        guess = lax.dot_general(hidden, weight(2), (((1,), (1,)), ((), ())), preferred_element_type=f32)
        scale = jnp.broadcast_to(rate[head, pl.ds(slot, 1)], (depth, tokens)).T
        error = (scale * (guess - v[j].astype(f32))).astype(bf16)
        back = jnp.dot(error, weight(2), preferred_element_type=f32)
        d_gate = (back * value * sig * (1.0 + gate * (1.0 - sig))).astype(bf16)
        d_up = (back * gate * sig).astype(bf16)
        key_t, err_t = rows_in.T, error.T
        for m, (left, right) in enumerate(((key_t, d_gate), (key_t, d_up), (err_t, hidden))):
            term = jnp.dot(left, right, preferred_element_type=f32)
            grad[j, m] = term.reshape(grad.shape[2:])
            copy(TERMS[m], j).start()

    def queries(j):
        depth, head = q.shape[2], j % heads

        def weight(m):
            return w[j, m].reshape(depth, w.shape[6])

        gate = jnp.dot(q[j], weight(0), preferred_element_type=f32)
        value = jnp.dot(q[j], weight(1), preferred_element_type=f32)
        hidden = (gate * jax.nn.sigmoid(gate) * value).astype(bf16)
        applied = lax.dot_general(hidden, weight(2), (((1,), (1,)), ((), ())), preferred_element_type=f32)
        mean = jnp.mean(applied * applied, axis=-1, keepdims=True)
        normed = applied * lax.rsqrt(mean + epsilon) * gain[pl.ds(head, 1)]
        out_ref[j] = normed.astype(bf16)

    def chip(j):
        need(j, CHIP)
        for m in range(3):
            acc[j, m] = (grad[j, m, :, :, c] + land_c[j, m]).astype(bf16)

    def landed(j, name, which):
        first, size = PLACE[name]
        skip = 1 if which == REST and size == 3 else 0
        return land[j, pl.ds(first + skip, SIZE[which])].astype(f32)

    def add(j, name):
        px, py, rows_of, terms = ADD[name]
        need(j, name)
        sum_at = (column[px], ring[py], part[rows_of])
        split = terms[1][1] if len(terms) == 2 else None
        for which in (GATE, REST) if split else (ALL,):
            at = (j, mats[which], column[px], ring[py])
            mine = grad[at + (c, part[rows_of])] + land_c[at + (part[rows_of],)]
            total = mine + landed(j, terms[0][0], which)
            if which == split:
                total = total + landed(j, terms[1][0], which)
            acc[(j, mats[which]) + sum_at] = total.astype(bf16)

    def final(j, name):
        rows_of, terms = FINAL[name]
        need(j, name)
        total = grad[j, :, x, y, c, part[rows_of]] + land_c[j, :, x, y, part[rows_of]]
        for term in terms:
            total = total + landed(j, term, ALL)
        if j < heads:
            old = cur[j, :, part[rows_of]]
        else:
            came = w[j, :, x, y, c, part[rows_of]].astype(f32)
            old = jnp.where(g == 0, init[j - heads, :, part[rows_of]], came)
        new = old - total * (1.0 / float(q.shape[1] * 16))
        if j < heads:
            moved[j, :, part[rows_of]] = new.astype(bf16)
        else:
            state_out_ref[j - heads, :, part[rows_of]] = new

    def take(j, name):
        @pl.when(g > 0)
        def _():
            arrived(j - heads, name)

    passed_on = set()

    def pass_on(j, name):
        first = not passed_on
        passed_on.add(name)

        @pl.when(g < groups - 1)
        def _():
            if first:
                @pl.when(g == middle)
                def _():
                    pl.semaphore_wait(go_sem, 1)
            copy(name, j).start()

    started = set()

    def take_step(name, j):
        if name == KEYS:
            if not started:
                started.add(name)
                for one in loads[1:]:
                    one.wait()

                @pl.when(g == 0)
                def _():
                    for h in range(heads):
                        w[heads + h, :, x, y, c] = init[h].astype(bf16)

            compute(j)
        elif name == QUERIES:
            queries(j)
        elif name == CHIP:
            chip(j)
        elif name in ADD:
            add(j, name)
        elif name in FINAL:
            final(j, name)
        elif name in (ISA, ISB):
            take(j, SHIFT[name - ISA])
        elif name in SHIFT:
            pass_on(j, name)
        else:
            if name in GATHER:
                need(j, *GATHER[name][5])
            copy(name, j).start()

    def load(n, src, dst):
        return pltpu.make_async_copy(src, dst, in_sem.at[n])

    loads = [
        load(0, state_hbm, cur), load(1, q_hbm, q), load(2, k_hbm, k), load(3, v_hbm, v),
        load(4, rate_hbm, rate), load(5, init_hbm, init), load(6, gain_hbm, gain),
    ]
    for one in loads:
        one.start()
    barrier = pltpu.get_barrier_semaphore()

    def hello(other):
        pl.semaphore_signal(barrier, inc=1, device_id=other, device_id_type=MESH)

    for other in (up, down, pair, sib):
        hello(other)

    @pl.when((g > 0) & (g != middle + 1))
    def _():
        hello(behind)

    @pl.when((g == middle) | (g == middle + 1))
    def _():
        hello((groups - 1, jnp.where(g == middle, across, me)))

    loads[0].wait()
    for h in range(heads):
        w[h, :, x, y, c] = cur[h].astype(bf16)
    near = jnp.where(g == middle, 4, jnp.where(g == groups - 1, 6, 5))
    pl.semaphore_wait(barrier, near)

    @pl.when(g == groups - 1)
    def _():
        pl.semaphore_signal(go_sem, inc=1, device_id=(middle, across), device_id_type=MESH)

    for step in SCHEDULE:
        take_step(step // 6, step % 6)

    for j in range(jobs):
        blocks = land.at[:, pl.ds(0, SENT // jobs)]
        pltpu.make_async_remote_copy(
            src_ref=blocks, dst_ref=blocks, send_sem=send_sem.at[j], recv_sem=recv_sem.at[j, 0],
            device_id=sib, device_id_type=MESH,
        ).wait_send()

    @pl.when(g < groups - 1)
    def _():
        for h in range(heads):
            for name in SHIFT:
                copy(name, h).wait_send()


def on_device(queries, key_tokens, value_tokens, token_rate, state_in, init_state, norm_gain):
    slots, heads, tokens, depth = queries.shape
    rows, hidden = init_state.shape[1], init_state.shape[3]
    jobs = slots * heads
    groups = lax.axis_size("group")
    half = rows // 2
    state = jnp.transpose(state_in[0], (0, 2, 1, 3))
    init = jnp.transpose(init_state, (0, 2, 1, 3))
    any_spec, vmem = pl.BlockSpec(memory_space=pl.ANY), pl.BlockSpec(memory_space=pltpu.VMEM)
    V = pltpu.VMEM
    out, new = pl.pallas_call(
        functools.partial(kernel, heads, groups),
        out_shape=(
            pltpu.VMEM((jobs, tokens, depth), bf16),
            pltpu.VMEM((heads, 3, rows, hidden), f32),
        ),
        in_specs=[any_spec] * 7,
        out_specs=(vmem, vmem),
        scratch_shapes=[
            V((jobs, tokens, depth), bf16), V((jobs, tokens, depth), bf16), V((jobs, tokens, depth), bf16),
            V((heads, slots, tokens), f32), V((heads, 3, rows, hidden), f32), V((heads, depth), f32),
            V((heads, 3, rows, hidden), f32),
            V((jobs, 3, 2, 4, 2, rows, hidden), bf16), V((jobs, 3, 2, 4, 2, rows, hidden), f32),
            V((jobs, 3, 2, 4, rows, hidden), bf16), V((heads, 3, rows, hidden), bf16),
            V((jobs, 3, 2, 4, rows, hidden), f32), V((jobs, LANDED, half, hidden), bf16),
            pltpu.SemaphoreType.DMA((7,)), pltpu.SemaphoreType.DMA((jobs,)),
            pltpu.SemaphoreType.DMA((jobs, len(WAITS))), pltpu.SemaphoreType.DMA((heads, 2)),
            pltpu.SemaphoreType.REGULAR,
        ],
        compiler_params=pltpu.CompilerParams(
            collective_id=0, has_side_effects=True, vmem_limit_bytes=60 * 1024 * 1024
        ),
    )(
        queries.reshape(jobs, tokens, depth), key_tokens.reshape(jobs, tokens, depth),
        value_tokens.reshape(jobs, tokens, depth), jnp.transpose(token_rate, (1, 0, 2)), state, init,
        norm_gain,
    )
    return out.reshape(queries.shape), jnp.transpose(new, (0, 2, 1, 3))[None]


def solution(mesh):
    in_specs = (
        P(None, None, ("group", "shard"), None),
        P(None, None, ("group", "shard"), None),
        P(None, None, ("group", "shard"), None),
        P(None, None, ("group", "shard")),
        P("group", None, "shard", None, None),
        P(None, "shard", None, None),
        P(),
    )
    out_specs = (P(None, None, ("group", "shard"), None), P("group", None, "shard", None, None))
    return jax.shard_map(
        on_device, mesh=mesh, in_specs=in_specs, out_specs=out_specs, check_vma=False
    )
```

time: 92.7 us -> 88.8 us (0.958)
  Pallas kernels: 90.3 us -> 86 us
    pallas_call x1, Pallas kernels: 90.3 us -> 86 us  [on_device(): pl.pallas_call(functools.partial(kernel, heads, groups), out_shape=(pltpu...]
where the time goes in v3:
time: 88.8 us; the launch traced here: 88.3 us
  Pallas kernels  86 us (97%)
  local copies, waits for them, and re-layouts  1.7 us (2%)
    pallas_call x1, Pallas kernels, on_device(): pl.pallas_call(functools.partial(kernel, heads, groups), out_shape=(pltpu...  86 us

profile of v3, /device:TPU:10, one launch (start us, length us, event | category | flops | bytes accessed | tf_op | source)
XLA Modules:
  0.0 88.3 jit_solution(7301723683899530391)
XLA Ops:
  0.6 86.0 %shard_map.86 = (bf16[6,128,512]{2,1,0:T(8,128)(2,1)S(1)}, f32[3,3,32,512]{3,2,1,0:T(8,128)S(1)}) custom-call(bf16[6,128,512]{2,1,0:T(8,128)(2,1)} %bitcast.14, bf16[6,128,512]{2,1,0:T(8,128)(2,1)} %bitcast.15, bf16[6,128,512]{2,1,0:T(8,128)(2,1)} %bitcast.16, f32[3,2,128]{2,1,0:T(2,128)} %bitcast.19, f32[3,3,32,512]{3,2,1,0:T(8,128)} %bitcast.17, ...), custom_call_target="tpu_custom_call" | custom-call | tf_op jit(solution)/shard_map/pallas_call | solution.py:363
  86.6 0.9 copy.11
  87.5 0.8 copy.12
